TPU v7x, 256 devices: a whole 4x4x8 slice. The times are simulated.
256 devices in a mesh: row: 16 (over x, y_lo, core), col: 16 (over z, y_hi).
Axes of the slice: x: 4, y: 4 (y_hi: 2, y_lo: 2; y = y_hi * 2 + y_lo), z: 8, core: 2. Of those that a mesh axis runs over, the one named last changes fastest.
Arguments:
- ancestor_inverse: float32 [24576, 24576], P('row', 'col'), may hold values from -1 to 5, as said below
- factor_panel: float32 [24576, 512], P('row'), may hold values from -6 to 6
- ancestor_blocks: int32 [16, 12], replicated, may hold values from 0 to 11, each once within a row
- ancestor_count: int32 [16], replicated, may hold values from 1 to 12, 128 in all
Outputs:
- inverse_panel: float32 [24576, 512], P(('row', 'col'))
- inverse_row: float32 [512, 24576], P('row', 'col')
Inputs may be any that keep to these rules, and one draw needn't show every extreme that they name: ancestor_inverse is symmetric: equal to its transpose. `ancestor_blocks`: each row is an ordering of the 12 blocks of one tile. `ancestor_count`: the counts sum to 128, and some tile has all 12 slots live.
All inputs are finite; a program needn't handle non-finite values.
Results may differ from a plain program's by a relative error of at most 0.000071.
Values sent between devices are 32-bit elements; how exact they have to be, the bound alone decides.
No kernel may reach another device: no remote copies, remote signals or barrier semaphores. Data moves between devices by JAX's collectives and lax.ppermute only.
A program may use at most 128 MiB of HBM per device.

v0:
```python
import jax
import jax.numpy as jnp
from jax import lax
from jax.sharding import PartitionSpec as P

highest = lax.Precision.HIGHEST


def from_root(value, axis, source):
    kept = jnp.where(lax.axis_index(axis) == source, value, 0).astype(value.dtype)
    return lax.psum(kept, axis)


def slot_table(row_order, row_count, tile_blocks):
    slot_ids = lax.iota(jnp.int32, tile_blocks)
    active = slot_ids < row_count
    onehot = jnp.logical_and(row_order[:, None] == slot_ids[None, :], active[:, None])
    return (onehot.astype(jnp.float32), active)


def to_natural(panel_tile, onehot, block_rows):
    tile_blocks = onehot.shape[0]
    blocks = panel_tile.reshape(tile_blocks, block_rows, panel_tile.shape[1])
    placed = jnp.einsum("sj,sbw->jbw", onehot, blocks, precision=highest)
    return placed.reshape(tile_blocks * block_rows, panel_tile.shape[1])


def natural_index(row_order, active, block_rows, tile_start):
    within = lax.iota(jnp.int32, block_rows)
    positions = (tile_start + row_order[:, None] * block_rows + within[None, :]).reshape(-1)
    keep_mask = jnp.repeat(active.astype(jnp.float32), block_rows)
    return (positions, keep_mask)


def per_device(ancestor_inverse, factor_panel, ancestor_blocks, ancestor_count):
    row_devices = lax.axis_size("row")
    col_devices = lax.axis_size("col")
    per_column = row_devices // col_devices
    grid_row = lax.axis_index("row")
    grid_col = lax.axis_index("col")
    tile_rows = factor_panel.shape[0]
    super_width = factor_panel.shape[1]
    tile_blocks = ancestor_blocks.shape[1]
    block_rows = tile_rows // tile_blocks
    col_lists = []
    mask_lists = []
    source = grid_col * per_column + 0
    arrived = from_root(factor_panel, "row", source)
    row_order = lax.dynamic_index_in_dim(ancestor_blocks, source, 0, keepdims=False)
    row_count = lax.dynamic_index_in_dim(ancestor_count, source, 0, keepdims=False)
    onehot, active = slot_table(row_order, row_count, tile_blocks)
    panels = to_natural(arrived, onehot, block_rows)
    where_cols, keep_cols = natural_index(row_order, active, block_rows, 0)
    col_lists.append(where_cols)
    mask_lists.append(keep_cols)
    own_order = lax.dynamic_index_in_dim(ancestor_blocks, grid_row, 0, keepdims=False)
    own_count = lax.dynamic_index_in_dim(ancestor_count, grid_row, 0, keepdims=False)
    own_hot, own_active = slot_table(own_order, own_count, tile_blocks)
    row_positions, row_mask = natural_index(own_order, own_active, block_rows, 0)
    share_rows = tile_rows // col_devices
    picked = jnp.take(ancestor_inverse, row_positions, axis=0)
    product = jnp.dot(picked, panels, precision=highest, preferred_element_type=jnp.float32)
    inverse_panel = lax.psum_scatter(
        -product * row_mask[:, None], "col", scatter_dimension=0, tiled=True
    )
    moved = inverse_panel.T.reshape(super_width, 1, share_rows)
    mirrored = lax.all_to_all(
        lax.all_to_all(moved, "row", split_axis=0, concat_axis=1, tiled=True),
        "col",
        split_axis=1,
        concat_axis=2,
        tiled=True,
    )
    inverse_row = mirrored.reshape(super_width // row_devices, per_column * tile_rows)
    return (inverse_panel, inverse_row)


def solution(mesh):
    placed = (P("row", "col"), P("row", None), P(), P())
    return jax.shard_map(
        per_device,
        mesh=mesh,
        in_specs=placed,
        out_specs=(P(("row", "col"), None), P("row", "col")),
        check_vma=False,
    )
```

profile of v0, /device:TPU:1, one launch (start us, length us, event | category | flops | bytes accessed | tf_op | source)
XLA Modules:
  0.0 428.5 jit_solution(5537427536059488078)
XLA Ops:
  7.2 0.0 all-reduce.2.cloned.1.call-start
  7.2 0.4 broadcast_select_fusion
  7.6 3.8 copy.14
  11.4 0.0 all-reduce.2.cloned.1.call-update
  11.4 0.0 reduce-scatter.2.cloned.1.call-start
  11.5 0.8 multiply_bitcast_fusion
  12.2 0.1 fusion.10
  12.4 14.1 %gather_fusion = f32[1536,1536]{1,0:T(8,128)} fusion(f32[1536,1536]{1,0:T(8,128)} %param.4, s32[2048]{0:T(1024)S(1)} %pad_clamp_fusion), kind=kCustom, calls=%fused_computation | custom fusion | bytes 18880512 | tf_op jit(solution)/shard_map/jit(_take)/gather | solution.py:61
  26.5 0.6 fusion.22
  27.1 0.6 compare_convert_fusion
  27.7 0.7 iota_compare_fusion.1
  28.4 0.1 fusion.13
  28.5 0.1 broadcast_bitcast_fusion
  28.5 123.2 %all-reduce.2.cloned.1.call-done = f32[12,128,512]{2,0,1:T(8,128)} async-done(((f32[12,128,512]{2,0,1:T(8,128)}), f32[12,128,512]{2,0,1:T(8,128)}) %all-reduce.2.cloned.1.call-update) | async-done | bytes 3145744 | tf_op jit(solution)/shard_map/psum | solution.py:11
  151.7 4.4 %fusion.16 = f32[12,128,512]{2,0,1:T(8,128)S(1)} fusion(f32[12,128,512]{2,0,1:T(8,128)} %all-reduce.2.cloned.1.call-done, s32[12]{0:T(128)S(1)} %get-tuple-element.3, pred[12]{0:T(512)(128)(4,1)S(1)} %iota_compare_fusion.1), kind=kOutput, calls=%fused_computation.19 | convolution fusion | flops 113246496 | bytes 6291516 | tf_op jit(solution)/shard_map/sj,sbw->jbw/dot_general | solution.py:24
  156.2 1.8 copy.15
  158.0 17.1 %fusion.7 = f32[1536,512]{1,0:T(8,128)} fusion(f32[1536,512]{1,0:T(8,128)S(1)} %bitcast.40, f32[1536,1536]{1,0:T(8,128)S(1)} %copy-done, pred[1536]{0:T(1024)(128)(4,1)S(1)} %fusion.13, f32[1536]{0:T(1024)S(1)} %broadcast_bitcast_fusion), kind=kOutput, calls=%fused_computation.6 | convolution fusion | flops 14499446784 | bytes 15736320 | tf_op jit(solution)/shard_map/dot_general | solution.py:62
  175.2 0.0 reduce-scatter.2.cloned.1.call-update
  175.2 209.3 %reduce-scatter.2.cloned.1.call-done = f32[96,512]{1,0:T(8,128)} async-done(((f32[1536,512]{1,0:T(8,128)}), f32[96,512]{1,0:T(8,128)}) %reduce-scatter.2.cloned.1.call-update) | async-done | bytes 196624 | tf_op jit(solution)/shard_map/reduce_scatter | solution.py:63
  384.4 1.0 copy.16
  385.5 16.2 %all_to_all.27 = f32[512,1,96]{2,1,0:T(1,128)S(1)} all-to-all(f32[512,1,96]{2,1,0:T(1,128)S(1)} %copy.16), channel_id=1, replica_groups=mesh['row'=16,'col'=16] {'row'}, dimensions={0} | all-to-all | bytes 393216 | tf_op jit(solution)/shard_map/all_to_all | solution.py:68
  401.7 19.0 %all_to_all.28 = f32[32,16,96]{2,0,1:T(8,128)S(1)} all-to-all(f32[32,16,96]{2,0,1:T(8,128)S(1)} %bitcast.41), channel_id=1, replica_groups=mesh['row'=16,'col'=16] {'col'}, dimensions={1} | all-to-all | bytes 393216 | tf_op jit(solution)/shard_map/all_to_all | solution.py:67
  420.7 0.2 copy.17
  420.8 0.8 reshape.79
  (6 shorter events, 0.0 us)
Async XLA Ops:
  7.2 144.6 %all-reduce.2.cloned.1.call-start = ((), (), s32[]{:S(2)}) async-start(), calls=%async_computation.3 | async-start | bytes 8388608 | tf_op jit(solution)/shard_map/psum | solution.py:11
  11.4 373.0 %reduce-scatter.2.cloned.1.call-start = ((), (), s32[]{:S(2)}) async-start(), calls=%async_computation.4 | async-start | bytes 3342336 | tf_op jit(solution)/shard_map/reduce_scatter | solution.py:63
  12.4 14.1 %copy-start.1 = (s32[16]{0:T(128)S(1)}, s32[16]{0:T(128)}, u32[]{:S(2)}) copy-start(s32[16]{0:T(128)} %param.7) | copy-start | bytes 196
  151.7 6.3 %copy-start = (f32[1536,1536]{1,0:T(8,128)S(1)}, f32[1536,1536]{1,0:T(8,128)}, u32[]{:S(2)}) copy-start(f32[1536,1536]{1,0:T(8,128)} %gather_fusion) | copy-start | bytes 28311556
Sparse Core Ops, SparseCore 0:
  11.5 140.1 all-reduce.1
  175.3 209.0 reduce-scatter.1
where the time goes:
time: 429 us; the launch traced here: 428 us
  waiting for transfers between devices  333 us (78%)
  blocking collectives  35.2 us (8%)
  local copies, waits for them, and re-layouts  22.4 us (5%)
  matrix products  21.6 us (5%)
  between operations  14.1 us (3%)
    reduce_scatter x1, waiting for transfers between devices, per_device(): lax.psum_scatter(-product * row_mask[:, None], 'col', scatter_dimension=0...  209 us
    psum x1, waiting for transfers between devices, from_root(): return lax.psum(kept, axis)  123 us
    all_to_all x1, blocking collectives, per_device(): lax.all_to_all(lax.all_to_all(moved, 'row', split_axis=0, concat_axis=1,...  19 us
    dot_general x1, matrix products, per_device(): jnp.dot(picked, panels, precision=highest, preferred_element_type=jnp.flo...  17.1 us
    all_to_all x1, blocking collectives, per_device(): lax.all_to_all(moved, 'row', split_axis=0, concat_axis=1, tiled=True)  16.2 us
    gather x1, local copies, waits for them, and re-layouts, per_device(): picked = jnp.take(ancestor_inverse, row_positions, axis=0)  14.1 us
  transfers between devices with their start and end apart: 2, of which 2 were waited for; matrix products, arithmetic and copies ran while one was open for 4% of the time, Pallas kernels for 0%

commit v1 on v0

--- a/solution.py
+++ b/solution.py
@@ -8,7 +8,7 @@
 
 def from_root(value, axis, source):
     kept = jnp.where(lax.axis_index(axis) == source, value, 0).astype(value.dtype)
-    return lax.psum(kept, axis)
+    return jnp.sum(lax.all_gather(kept, axis), axis=0)
 
 
 def slot_table(row_order, row_count, tile_blocks):

time: 429 us -> 561 us (1.31)
  waiting for transfers between devices: 333 us -> 449 us
  other arithmetic: 2.63 us -> 22.8 us
    all_gather x0 -> x1, waiting for transfers between devices: none -> 241 us  [from_root(): return jnp.sum(lax.all_gather(kept, axis), axis=0)]
    psum x1 -> x0, waiting for transfers between devices: 123 us -> none  [from_root(): return lax.psum(kept, axis)]
    reduce_sum x0 -> x1, other arithmetic: none -> 18.6 us  [from_root(): return jnp.sum(lax.all_gather(kept, axis), axis=0)]
  transfers between devices with their start and end apart: 2 -> 2, of which waited for: 2 -> 2; matrix products, arithmetic and copies ran while one was open for 4% -> 3% of each run, Pallas kernels for 0% -> 0%
where the time goes in v1:
time: 561 us
  waiting for transfers between devices  449 us (80%)
  blocking collectives  35.3 us (6%)
  other arithmetic  22.8 us (4%)
  matrix products  21.1 us (4%)
  local copies, waits for them, and re-layouts  18.5 us (3%)
  between operations  14.1 us (3%)
    all_gather x1, waiting for transfers between devices, from_root(): return jnp.sum(lax.all_gather(kept, axis), axis=0)  241 us
    reduce_scatter x1, waiting for transfers between devices, per_device(): lax.psum_scatter(-product * row_mask[:, None], 'col', scatter_dimension=0...  208 us
    all_to_all x1, blocking collectives, per_device(): lax.all_to_all(lax.all_to_all(moved, 'row', split_axis=0, concat_axis=1,...  19.1 us
    reduce_sum x1, other arithmetic, from_root(): return jnp.sum(lax.all_gather(kept, axis), axis=0)  18.6 us
    dot_general x1, matrix products, per_device(): jnp.dot(picked, panels, precision=highest, preferred_element_type=jnp.flo...  17.2 us
    all_to_all x1, blocking collectives, per_device(): lax.all_to_all(moved, 'row', split_axis=0, concat_axis=1, tiled=True)  16.1 us
    gather x1, local copies, waits for them, and re-layouts, per_device(): picked = jnp.take(ancestor_inverse, row_positions, axis=0)  14 us
  transfers between devices with their start and end apart: 2, of which 2 were waited for; matrix products, arithmetic and copies ran while one was open for 3% of the time, Pallas kernels for 0%

profile of v1, /device:TPU:1, one launch (start us, length us, event | category | flops | bytes accessed | tf_op | source)
XLA Modules:
  0.0 560.8 jit_solution(15582330299241973841)
XLA Ops:
  7.2 0.0 all-gather.3.cloned.1.call-start
  7.2 2.0 broadcast_select_fusion
  9.2 0.0 all-gather.3.cloned.1.call-update
  9.2 0.0 reduce-scatter.2.cloned.1.call-start
  9.3 0.8 multiply_bitcast_fusion
  10.0 0.1 fusion.12
  10.2 14.0 %gather_fusion = f32[1536,1536]{1,0:T(8,128)} fusion(f32[1536,1536]{1,0:T(8,128)} %param.4, s32[2048]{0:T(1024)S(1)} %pad_clamp_fusion), kind=kCustom, calls=%fused_computation | custom fusion | bytes 18880512 | tf_op jit(solution)/shard_map/jit(_take)/gather | solution.py:61
  24.2 0.6 fusion.23
  24.8 0.6 iota_compare_fusion.1
  25.5 0.7 compare_convert_fusion
  26.1 0.1 fusion.15
  26.2 0.1 broadcast_bitcast_fusion
  26.3 240.8 %all-gather.3.cloned.1.call-done = f32[24576,512]{1,0:T(8,128)} async-done(((f32[1536,512]{1,0:T(8,128)}), f32[24576,512]{1,0:T(8,128)}) %all-gather.3.cloned.1.call-update) | async-done | bytes 50331664 | tf_op jit(solution)/shard_map/all_gather | solution.py:11
  267.1 18.6 %reduce_sum.9 = f32[1536,512]{1,0:T(8,128)S(1)} reduce(f32[16,1536,512]{2,1,0:T(8,128)} %bitcast.39, f32[]{:T(128)} %constant.41.clone.1), dimensions={0}, to_apply=%region_0.1 | reduce | flops 11796480 | bytes 53477380 | tf_op jit(solution)/shard_map/reduce_sum | solution.py:11
  285.7 3.9 fusion.4
  289.5 1.8 copy.15
  291.4 17.2 %fusion.9 = f32[1536,512]{1,0:T(8,128)} fusion(f32[1536,512]{1,0:T(8,128)S(1)} %bitcast.41, f32[1536,1536]{1,0:T(8,128)S(1)} %copy-done, pred[1536]{0:T(1024)(128)(4,1)S(1)} %fusion.15, f32[1536]{0:T(1024)S(1)} %broadcast_bitcast_fusion), kind=kOutput, calls=%fused_computation.8 | convolution fusion | flops 14499446784 | bytes 15736320 | tf_op jit(solution)/shard_map/dot_general | solution.py:62
  308.6 0.0 reduce-scatter.2.cloned.1.call-update
  308.6 208.1 %reduce-scatter.2.cloned.1.call-done = f32[96,512]{1,0:T(8,128)} async-done(((f32[1536,512]{1,0:T(8,128)}), f32[96,512]{1,0:T(8,128)}) %reduce-scatter.2.cloned.1.call-update) | async-done | bytes 196624 | tf_op jit(solution)/shard_map/reduce_scatter | solution.py:63
  516.7 1.0 copy.16
  517.7 16.1 %all_to_all.27 = f32[512,1,96]{2,1,0:T(1,128)S(1)} all-to-all(f32[512,1,96]{2,1,0:T(1,128)S(1)} %copy.16), channel_id=1, replica_groups=mesh['row'=16,'col'=16] {'row'}, dimensions={0} | all-to-all | bytes 393216 | tf_op jit(solution)/shard_map/all_to_all | solution.py:68
  533.9 19.1 %all_to_all.28 = f32[32,16,96]{2,0,1:T(8,128)S(1)} all-to-all(f32[32,16,96]{2,0,1:T(8,128)S(1)} %bitcast.42), channel_id=1, replica_groups=mesh['row'=16,'col'=16] {'col'}, dimensions={1} | all-to-all | bytes 393216 | tf_op jit(solution)/shard_map/all_to_all | solution.py:67
  553.0 0.2 copy.17
  553.2 0.8 reshape.79
  (6 shorter events, 0.0 us)
Async XLA Ops:
  7.2 259.9 %all-gather.3.cloned.1.call-start = ((), (), s32[]{:S(2)}) async-start(), calls=%async_computation.4 | async-start | bytes 53477376 | tf_op jit(solution)/shard_map/all_gather | solution.py:11
  9.2 507.5 %reduce-scatter.2.cloned.1.call-start = ((), (), s32[]{:S(2)}) async-start(), calls=%async_computation.3 | async-start | bytes 3342336 | tf_op jit(solution)/shard_map/reduce_scatter | solution.py:63
  10.2 14.0 %copy-start.1 = (s32[16]{0:T(128)S(1)}, s32[16]{0:T(128)}, u32[]{:S(2)}) copy-start(s32[16]{0:T(128)} %param.7) | copy-start | bytes 196
  285.7 5.7 %copy-start = (f32[1536,1536]{1,0:T(8,128)S(1)}, f32[1536,1536]{1,0:T(8,128)}, u32[]{:S(2)}) copy-start(f32[1536,1536]{1,0:T(8,128)} %gather_fusion) | copy-start | bytes 28311556
Sparse Core Ops, SparseCore 0:
  9.8 257.2 all-gather.2
  308.7 207.8 reduce-scatter.1
